TPU v7x, 32 devices: a whole 2x2x4 slice. The times are simulated.
32 devices in a mesh: rows: 4 (over y, core), cols: 8 (over z, x).
Axes of the slice: x: 2, y: 2, z: 4, core: 2. Of those that a mesh axis runs over, the one named last changes fastest.
Arguments:
- prior: float32 [64, 512, 512], P('rows', 'cols'), may hold values from -6 to 6
- obs_cell: int32 [8, 128], replicated, may hold values from 0 to 32767, as said below
- obs_weight: float32 [8, 128, 8], replicated, may hold values from 0.1 to 1
- obs_value: float32 [8, 128], replicated, may hold values from -8 to 8
- obs_var: float32 [8, 128], replicated, may hold values from 0.25 to 4
- loc_mask: int32 [8, 32], replicated, may hold values from 0 to 1, as said below
- batch_order: int32 [8], replicated, may hold values from 0 to 7, each once
- kernel: float32 [8, 7, 7], replicated, may hold values from 0.005 to 0.04
- mixing: float32 [8, 8], replicated, may hold values from -2 to 2
Outputs:
- forecast: float32 [64, 512, 512], P('rows', 'cols')
Inputs may be any that keep to these rules, and one draw needn't show every extreme that they name: `obs_cell`: all 128 cells of one batch lie in one tile, rows r * 16 to (r + 1) * 16 - 1 and columns c * 64 to (c + 1) * 64 - 1, whose index is r * 8 + c. `loc_mask`: for each batch the tiles marked 1 form a rectangle of tiles that contains the tile of that batch's cells. `batch_order`: each batch appears once.
All inputs are finite; a program needn't handle non-finite values.
Results may differ from a plain program's by a relative error of at most 0.0003.
Values sent between devices are 32-bit elements; how exact they have to be, the bound alone decides.
No kernel may reach another device: no remote copies, remote signals or barrier semaphores. Data moves between devices by JAX's collectives and lax.ppermute only.
A program may use at most 128 MiB of HBM per device.

v0:
```python
import functools

import jax
import jax.numpy as jnp
from jax import lax
from jax.experimental import pallas as pl
from jax.experimental.pallas import tpu as pltpu
from jax.sharding import PartitionSpec as P

BATCHES = 8
OBS = 128
SPECIES = 8
MEMBERS = 64
KW = 7
HALO = KW // 2
HALFW = 48
BF16 = jnp.bfloat16
F32 = jnp.float32
VMEM = pl.BlockSpec(memory_space=pltpu.VMEM)
SMEM = pl.BlockSpec(memory_space=pltpu.SMEM)
PARAMS = pltpu.CompilerParams(vmem_limit_bytes=56 << 20)


def split(x):
    high = x.astype(BF16)
    return high, (x - high.astype(F32)).astype(BF16)


def dot(a, b):
    return jnp.dot(a, b, preferred_element_type=F32)


def swap_halves(x):
    return pltpu.roll(x, MEMBERS, axis=x.ndim - 1)


def low_lanes(shape):
    return lax.broadcasted_iota(jnp.int32, shape, len(shape) - 1) < MEMBERS


def taper_weights(squared):
    inverse = lax.rsqrt(jnp.maximum(squared, 1e-4))
    ratio = squared * inverse
    inner = 1.0 - (ratio * ratio) * (5.0 / 3.0 - ratio * (0.625 + ratio * (0.5 - 0.25 * ratio)))
    left = jnp.maximum(2.0 - ratio, 0.0)
    left = left * left
    outer = (left * left) * (((ratio + 2.0) * ratio - 0.5) * (inverse * (1.0 / 12.0)))
    return jnp.where(ratio <= 1.0, inner, outer)


def gather_kernel(width, order, cells, weight_ref, prior_ref, kept_ref, sent_ref, picked):
    height, cols = prior_ref.shape[0], prior_ref.shape[1]
    my_row, my_col = lax.axis_index("rows"), lax.axis_index("cols")
    mine = 2 * lax.rem(my_row, 2) + lax.rem(lax.div(my_row, 2), 2)
    corner = my_row * height * width + my_col * cols
    kept_ref[...] = jnp.zeros_like(kept_ref)
    sent_ref[...] = jnp.zeros_like(sent_ref)
    for k in range(BATCHES):
        batch = order[k]
        first = cells[batch, 0]
        owner = (lax.div(first, width * height) == my_row) & (
            lax.div(lax.rem(first, width), cols) == my_col
        )

        @pl.when(owner)
        def _():
            def one(i, carry):
                cell = cells[batch, i] - corner
                row = lax.div(cell, width)
                picked[pl.ds(i, 1), :] = prior_ref[row, pl.ds(cell - row * width, 1), :]
                return carry

            lax.fori_loop(0, OBS, one, 0, unroll=8)
            weights = jnp.transpose(weight_ref[batch])
            low = low_lanes((OBS, 2 * MEMBERS))
            total = jnp.zeros((OBS, 2 * MEMBERS), F32)
            for p in range(SPECIES // 2):
                scale = jnp.where(low, weights[:, 2 * p : 2 * p + 1], weights[:, 2 * p + 1 : 2 * p + 2])
                total = total + scale * picked[:, 128 * p : 128 * (p + 1)]
            total = total + swap_halves(total)
            slot = jnp.bitwise_xor(k % 4, mine)
            keep = low if k < 4 else jnp.logical_not(low)

            @pl.when(slot < 2)
            def _():
                kept_ref[slot] = jnp.where(keep, total, kept_ref[slot])

            @pl.when(slot >= 2)
            def _():
                sent_ref[slot - 2] = jnp.where(keep, total, sent_ref[slot - 2])


def flip(x, axis, bit):
    return lax.ppermute(x, axis, [(i, i ^ bit) for i in range(lax.axis_size(axis))])


def swap(x, axis, start):
    size = lax.axis_size(axis)
    pairs_of = [(i, i + 1) for i in range(start, size - 1, 2)]
    return lax.ppermute(x, axis, pairs_of + [(j, i) for i, j in pairs_of])


def behind(x, earlier):
    return lax.optimization_barrier((x, earlier))[0]


def exchange(kept, sent, prior):
    height, cols = prior.shape[0], prior.shape[1]
    even_row = lax.rem(lax.axis_index("rows"), 2) == 0
    even_col = lax.rem(lax.axis_index("cols"), 2) == 0
    first, last = prior[:, :HALO], prior[:, cols - HALO :]
    kept = kept + flip(sent, "rows", 1)
    side1 = swap(behind(jnp.where(even_col, first, last), kept), "cols", 1)
    kept = kept[0] + flip(kept[1], "rows", 2)
    side0 = swap(behind(jnp.where(even_col, last, first), kept), "cols", 0)
    hops = [("rows", 1 << b) for b in range(2, lax.axis_size("rows").bit_length() - 1)]
    hops += [("cols", 1 << b) for b in range(lax.axis_size("cols").bit_length() - 1)]
    stages = [kept]
    for axis, bit in hops:
        stages.append(stages[-1] + flip(stages[-1], axis, bit))
    left = jnp.where(even_col, side1, side0)
    right = jnp.where(even_col, side0, side1)

    def strip(lo, hi):
        return jnp.concatenate([prior[lo:hi], left[lo:hi], right[lo:hi]], 1)

    top, bottom = strip(0, HALO), strip(height - HALO, height)
    rows1 = swap(behind(jnp.where(even_row, top, bottom), stages[-3]), "rows", 1)
    rows0 = swap(behind(jnp.where(even_row, bottom, top), stages[-2]), "rows", 0)
    kept = stages[-1]
    other = flip(kept, "rows", 2)
    parts = kept, other, flip(kept, "rows", 1), flip(other, "rows", 1)
    return (side0, side1, rows0, rows1), parts


def update(x, taper, spread_w, gain_w):
    high, low_part = split(x)
    c_high, c_low = split(dot(jnp.concatenate([high, low_part, high], 1), spread_w) * taper)
    both = dot(c_high, gain_w)
    lanes = 2 * MEMBERS
    return x + (both[:, :lanes] + both[:, lanes:] + dot(c_low, gain_w[:, :lanes]))


def pair_up(a, b):
    low = low_lanes(a.shape)
    return jnp.where(low, a, swap_halves(b)), jnp.where(low, swap_halves(a), b)


def forecast_kernel(
    width, order, cells, mask, kern, mix, cell_ref, value_ref, var_ref, prior_ref,
    side0_ref, side1_ref, rows0_ref, rows1_ref, p0, p1, p2, p3,
    out_ref, field, predicted, table, place, spread0, gain0, spread1, gain1, lines,
):
    height, cols = prior_ref.shape[0], prior_ref.shape[1]
    my_row, my_col = lax.axis_index("rows"), lax.axis_index("cols")
    down, across = lax.axis_size("rows"), lax.axis_size("cols")
    mine = 2 * lax.rem(my_row, 2) + lax.rem(lax.div(my_row, 2), 2)
    for rel, part in enumerate((p0, p1, p2, p3)):
        predicted[jnp.bitwise_xor(rel, mine)] = part[...]
    pairs = height // 2
    depth = cols + 8
    lanes = 2 * MEMBERS
    even_row = lax.rem(my_row, 2) == 0
    even_col = lax.rem(my_col, 2) == 0

    def put(j, p, lo, a, b):
        first, second = pair_up(a, b)
        field[j, 2 * p, lo : lo + a.shape[0], :] = first
        field[j, 2 * p + 1, lo : lo + a.shape[0], :] = second

    for j in range(pairs + 3):
        for t in range(SPECIES):
            field[j, t, cols:depth, :] = jnp.zeros((8, lanes), F32)
    for p in range(SPECIES // 2):
        at = slice(128 * p, 128 * (p + 1))

        def left(r):
            return jnp.where(even_col, side1_ref[r, :, at], side0_ref[r, :, at])

        def right(r):
            return jnp.where(even_col, side0_ref[r, :, at], side1_ref[r, :, at])

        def above(r, lo, hi):
            return jnp.where(even_row, rows1_ref[r, lo:hi, at], rows0_ref[r, lo:hi, at])

        def below(r, lo, hi):
            return jnp.where(even_row, rows0_ref[r, lo:hi, at], rows1_ref[r, lo:hi, at])

        for j in range(pairs):
            put(j, p, 0, prior_ref[2 * j, :, at], prior_ref[2 * j + 1, :, at])
            put(j, p, cols, left(2 * j), left(2 * j + 1))
            put(j, p, cols + HALO, right(2 * j), right(2 * j + 1))
        for lo, hi in ((0, cols), (cols, cols + 2 * HALO)):
            put(pairs, p, lo, above(1, lo, hi), above(2, lo, hi))
            put(pairs + 1, p, lo, below(0, lo, hi), below(1, lo, hi))
            put(pairs + 2, p, lo, above(0, lo, hi), below(2, lo, hi))
    batches = [order[k] for k in range(BATCHES)]
    tiles = []
    for k in range(BATCHES):
        first = cells[batches[k], 0]
        tiles.append(lax.div(first, width * height) * across + lax.div(lax.rem(first, width), cols))
        table[k : k + 1, :] = cell_ref[pl.ds(batches[k], 1), :].astype(F32)
        table[8 + k : 9 + k, :] = value_ref[pl.ds(batches[k], 1), :]
        table[16 + k : 17 + k, :] = var_ref[pl.ds(batches[k], 1), :]
    cell_lane = table[0:8, :]
    row_lane = jnp.floor(cell_lane * (1.0 / width))
    col_lane = (cell_lane - row_lane * width) * (1.0 / HALFW)
    row_lane = row_lane * (1.0 / HALFW)
    row_col = jnp.transpose(row_lane)
    col_col = jnp.transpose(col_lane)
    value_col = jnp.transpose(table[8:16, :])
    var_col = jnp.transpose(table[16:24, :])
    low_obs = low_lanes((OBS, 2 * MEMBERS))
    index = lax.broadcasted_iota(jnp.int32, (depth, OBS), 0)
    to_left = (index >= cols) & (index < cols + HALO)
    to_right = index >= cols + HALO
    x_pos = jnp.where(to_left, index - cols - HALO, jnp.where(to_right, index - HALO, index))
    x_pos = (x_pos + my_col * cols).astype(F32) * (1.0 / HALFW)
    top_row = my_row * height
    zones = (
        jnp.maximum(my_row - 1, 0) * across, my_row * across, jnp.minimum(my_row + 1, down - 1) * across
    )
    sides = (jnp.maximum(my_col - 1, 0), my_col, jnp.minimum(my_col + 1, across - 1))
    row_pairs = [((top_row + 2 * j, 1), (top_row + 2 * j + 1, 1)) for j in range(pairs)]
    row_pairs += [
        ((top_row - 2, 0), (top_row - 1, 0)),
        ((top_row + height, 2), (top_row + height + 1, 2)),
        ((top_row - 3, 0), (top_row + height + 2, 2)),
    ]

    place[0:8, :] = row_lane
    place[8:16, :] = col_lane
    lane_index = lax.broadcasted_iota(jnp.int32, (OBS, BATCHES), 1)

    def column(values, k):
        return jnp.sum(jnp.where(lane_index == k, values, 0.0), axis=1, keepdims=True)

    def factors(k, spread_ref, gain_ref):
        block = predicted[lax.rem(k, 4)]
        turned_block = swap_halves(block)
        first_half = k < 4
        here = jnp.where(
            low_obs,
            jnp.where(first_half, block, turned_block),
            jnp.where(first_half, turned_block, block),
        )
        mean = jnp.sum(here, axis=1, keepdims=True) * (0.5 / MEMBERS)
        spread = here - mean
        variance = jnp.sum(spread * spread, axis=1, keepdims=True) * (0.5 / (MEMBERS - 1))
        var = column(var_col, k)
        denominator = variance + var
        shrink = 1.0 / (1.0 + jnp.sqrt(var / denominator))
        gain = ((column(value_col, k) - mean) - shrink * spread) / (denominator * (MEMBERS - 1))
        turned = jnp.transpose(spread)
        top = lax.broadcasted_iota(jnp.int32, turned.shape, 0) < MEMBERS
        zero = jnp.zeros_like(turned)
        wide = jnp.concatenate([jnp.where(top, turned, zero), jnp.where(top, zero, turned)], 1)
        wide_hi, wide_lo = split(wide)
        spread_ref[...] = jnp.concatenate([wide_hi, wide_hi, wide_lo], 0)
        tall = jnp.concatenate([jnp.where(low_obs, gain, zero), jnp.where(low_obs, zero, gain)], 0)
        gain_ref[...] = jnp.concatenate(split(tall), 1)

    def assimilate(k, spread_ref, gain_ref, next_spread_ref, next_gain_ref):
        batch = order[k]
        spread_w, gain_w = spread_ref[...], gain_ref[...]
        obs_row, obs_col = place[pl.ds(k, 1), :], place[pl.ds(8 + k, 1), :]
        for q in range(4):
            halves = []
            for later in (q, q + 4):
                dr = row_col[:, later : later + 1] - obs_row
                dc = col_col[:, later : later + 1] - obs_col
                on = (mask[batch, tiles[later]] > 0).astype(F32)
                halves.append(taper_weights(dr * dr + dc * dc) * on)
            predicted[q] = update(predicted[q], jnp.concatenate(halves, 1), spread_w, gain_w)
        factors(jnp.minimum(k + 1, BATCHES - 1), next_spread_ref, next_gain_ref)
        gap = x_pos - obs_col
        gap = gap * gap
        active = []
        for zone in zones:
            on = [(mask[batch, zone + side] > 0).astype(F32) for side in sides]
            active.append(jnp.where(to_left, on[0], jnp.where(to_right, on[2], on[1])))
        flat = (SPECIES * depth, lanes)
        for j in range(pairs + 3):
            halves = []
            for position, zone in row_pairs[j]:
                dy = position.astype(F32) * (1.0 / HALFW) - obs_row
                halves.append(taper_weights(gap + dy * dy) * active[zone])
            taper = jnp.concatenate([jnp.concatenate(halves, 1)] * SPECIES, 0)
            new = update(field[j].reshape(flat), taper, spread_w, gain_w)
            field[j] = new.reshape(SPECIES, depth, lanes)

    factors(jnp.int32(0), spread0, gain0)

    def two(i, carry):
        assimilate(2 * i, spread0, gain0, spread1, gain1)
        assimilate(2 * i + 1, spread1, gain1, spread0, gain0)
        return carry

    lax.fori_loop(0, BATCHES // 2, two, 0)

    sources = [pairs + 2, pairs] + list(range(pairs)) + [pairs + 1, pairs + 2]
    column = lax.broadcasted_iota(jnp.int32, (cols, 3 * depth), 1)
    third = column >= 2 * depth
    column = jnp.where(third, column - 2 * depth, jnp.where(column >= depth, column - depth, column))
    column = jnp.where(
        column < cols, column, jnp.where(column < cols + HALO, column - cols - HALO, column - HALO)
    )
    offset = column - lax.broadcasted_iota(jnp.int32, (cols, 3 * depth), 0) + HALO
    low = low_lanes((cols, lanes))

    def species(t, carry):
        bands = []
        for a in range(KW):
            band = jnp.zeros((cols, 3 * depth), F32)
            for e in range(KW):
                band = jnp.where(offset == e, kern[t, a * KW + e], band)
            high = band.astype(BF16).astype(F32)
            bands.append(jnp.where(third, band - high, high).astype(BF16))
        band = jnp.concatenate(bands, 0)
        for d in range(0, pairs + 4, 2):
            pieces = []
            for q in (d, d + 1):
                piece = field[sources[q], t]
                pieces.append(swap_halves(piece) if q in (0, pairs + 3) else piece)
            data = jnp.concatenate(pieces, 1)
            high = data.astype(BF16).astype(F32)
            data = jnp.concatenate([high, data - high, high], 0).astype(BF16)
            product = dot(band, data)
            lines[d] = product[:, :lanes]
            lines[d + 1] = product[:, lanes:]

        def part(q, a):
            return lines[q, a * cols : (a + 1) * cols, :]

        def odd(u):
            return swap_halves(part(u, 0) + part(u + 1, 2) + part(u + 2, 4) + part(u + 3, 6))

        before = odd(0)
        for j in range(pairs):
            after = odd(j + 1)
            straight = part(j + 1, 1) + part(j + 2, 3) + part(j + 3, 5)
            field[j, t, 0:cols, :] = straight + jnp.where(low, before, after)
            before = after
        return carry

    lax.fori_loop(0, SPECIES, species, 0)

    def mixed(j, carry):
        smooth = [field[j, t, 0:cols, :] for t in range(SPECIES)]
        for p in range(SPECIES // 2):
            total = []
            for s in (2 * p, 2 * p + 1):
                acc = mix[s, 0] * smooth[0]
                for t in range(1, SPECIES):
                    acc = acc + mix[s, t] * smooth[t]
                total.append(acc)
            out_ref[2 * j, :, 128 * p : 128 * (p + 1)] = jnp.where(low, total[0], swap_halves(total[1]))
            out_ref[2 * j + 1, :, 128 * p : 128 * (p + 1)] = jnp.where(
                low, swap_halves(total[0]), total[1]
            )
        return carry

    lax.fori_loop(0, pairs, mixed, 0)


def shards(prior, obs_cell, obs_weight, obs_value, obs_var, loc_mask, batch_order, kernel, mixing):
    height, cols, channels = prior.shape
    across = lax.axis_size("cols")
    width = cols * across
    pairs = height // 2
    lanes = 2 * MEMBERS
    kept, sent = pl.pallas_call(
        functools.partial(gather_kernel, width),
        out_shape=(jax.ShapeDtypeStruct((2, OBS, lanes), F32),) * 2,
        in_specs=[SMEM, SMEM, VMEM, VMEM],
        out_specs=(VMEM, VMEM),
        scratch_shapes=[pltpu.VMEM((OBS, channels), F32)],
        compiler_params=PARAMS,
        name="gather",
    )(batch_order, obs_cell, jnp.transpose(obs_weight, (0, 2, 1)), prior)
    halo, parts = exchange(kept, sent, prior)
    return pl.pallas_call(
        functools.partial(forecast_kernel, width),
        out_shape=jax.ShapeDtypeStruct((height, cols, channels), F32),
        in_specs=[SMEM] * 5 + [VMEM] * 12,
        out_specs=VMEM,
        scratch_shapes=[
            pltpu.VMEM((pairs + 3, SPECIES, cols + 8, lanes), F32),
            pltpu.VMEM((4, OBS, lanes), F32),
            pltpu.VMEM((24, OBS), F32),
            pltpu.VMEM((16, OBS), F32),
            pltpu.VMEM((3 * lanes, 2 * OBS), BF16),
            pltpu.VMEM((2 * OBS, 2 * lanes), BF16),
            pltpu.VMEM((3 * lanes, 2 * OBS), BF16),
            pltpu.VMEM((2 * OBS, 2 * lanes), BF16),
            pltpu.VMEM((pairs + 4, KW * cols, lanes), F32),
        ],
        compiler_params=PARAMS,
        name="forecast",
    )(
        batch_order, obs_cell, loc_mask, kernel.reshape(SPECIES, KW * KW), mixing,
        obs_cell, obs_value, obs_var, prior, *halo, *parts,
    )


def solution(mesh):
    return jax.shard_map(
        shards,
        mesh=mesh,
        in_specs=(P("rows", "cols", None), P(), P(), P(), P(), P(), P(), P(), P()),
        out_specs=P("rows", "cols", None),
        check_vma=False,
    )
```

profile of v0, /device:TPU:9, one launch (start us, length us, event | category | flops | bytes accessed | tf_op | source)
XLA Modules:
  0.0 84.9 jit_solution(3272344258952972934)
XLA Ops:
  0.0 2.6 %gather.1 = (f32[2,128,128]{2,1,0:T(8,128)}, f32[2,128,128]{2,1,0:T(8,128)}) custom-call(s32[8]{0:T(128)} %order.3, s32[8,128]{1,0:T(8,128)} %cell_ref.1, f32[8,8,128]{2,1,0:T(8,128)} %bitcast.7, f32[16,64,512]{2,1,0:T(8,128)} %prior_ref.3), custom_call_target="tpu_custom_call" | custom-call | tf_op jit(solution)/shard_map/gather/pallas_call | solution.py:372
  2.6 0.7 collective-permute-start
  3.3 1.2 %collective-permute-done = f32[2,128,128]{2,1,0:T(8,128)S(1)} collective-permute-done((f32[2,128,128]{2,1,0:T(8,128)}, f32[2,128,128]{2,1,0:T(8,128)S(1)}, u32[]{:S(2)}, u32[]{:S(2)}) %collective-permute-start) | collective-permute-done | bytes 131104 | tf_op jit(solution)/shard_map/ppermute | solution.py:94
  4.5 0.9 %add.15 = f32[2,128,128]{2,1,0:T(8,128)S(1)} add(f32[2,128,128]{2,1,0:T(8,128)} %get-tuple-element.11, f32[2,128,128]{2,1,0:T(8,128)S(1)} %collective-permute-done) | non-fusion elementwise | flops 32768 | bytes 393216 | tf_op jit(solution)/shard_map/add | solution.py:112
  5.4 4.1 %collective-permute-start.1 = (f32[128,128]{1,0:T(8,128)S(1)}, f32[128,128]{1,0:T(8,128)S(1)}, u32[]{:S(2)}, u32[]{:S(2)}) collective-permute-start(f32[128,128]{1,0:T(8,128)S(1)} %slice_bitcast_fusion), channel_id=1, source_target_pairs={{0,16},{8,24},{16,0},{24,8},{1,17},{9,25},{17,1},{25,9},{2,18},{10... | collective-permute-start | bytes 196616 | tf_op jit(solution)/shard_map/ppermute | solution.py:94
  9.5 0.1 slice_select_fusion
  9.6 1.9 %collective-permute-start.3 = (f32[16,3,512]{2,1,0:T(4,128)S(1)}, f32[16,3,512]{2,1,0:T(4,128)S(1)}, u32[]{:S(2)}, u32[]{:S(2)}) collective-permute-start(f32[16,3,512]{2,1,0:T(4,128)S(1)} %get-tuple-element.14), channel_id=1, source_target_pairs={{1,2},{3,4},{5,6},{2,1},{4,3},{6,5},{9,10},{11,12},{13,14},{10,9},... | collective-permute-start | bytes 294920 | tf_op jit(solution)/shard_map/ppermute | solution.py:100
  11.5 0.2 collective-permute-done.1
  11.7 1.0 %collective-permute-start.4 = (f32[128,128]{1,0:T(8,128)S(1)}, f32[128,128]{1,0:T(8,128)S(1)}, u32[]{:S(2)}, u32[]{:S(2)}) collective-permute-start(f32[128,128]{1,0:T(8,128)S(1)} %fusion.2), channel_id=1, source_target_pairs={{0,1},{1,0},{2,3},{3,2},{4,5},{5,4},{6,7},{7,6},{8,9},{9,8},{10,11... | collective-permute-start | bytes 196616 | tf_op jit(solution)/shard_map/ppermute | solution.py:94
  12.7 0.6 collective-permute-start.2
  13.2 0.1 fusion.3
  13.3 3.5 %collective-permute-done.4 = f32[128,128]{1,0:T(8,128)S(1)} collective-permute-done((f32[128,128]{1,0:T(8,128)S(1)}, f32[128,128]{1,0:T(8,128)S(1)}, u32[]{:S(2)}, u32[]{:S(2)}) %collective-permute-start.4) | collective-permute-done | bytes 65568 | tf_op jit(solution)/shard_map/ppermute | solution.py:94
  16.8 0.5 collective-permute-start.5
  17.3 3.5 %collective-permute-done.2.side0_ref = f32[16,3,512]{2,1,0:T(4,128)S(1)} collective-permute-done((f32[16,3,512]{2,1,0:T(4,128)S(1)}, f32[16,3,512]{2,1,0:T(4,128)S(1)}, u32[]{:S(2)}, u32[]{:S(2)}) %collective-permute-start.2) | collective-permute-done | bytes 98336 | tf_op jit(solution)/shard_map/ppermute | solution.py:100
  20.9 0.1 fusion
  21.0 3.7 %collective-permute-start.7 = (f32[3,70,512]{2,1,0:T(8,128)S(1)}, f32[3,70,512]{2,1,0:T(8,128)S(1)}, u32[]{:S(2)}, u32[]{:S(2)}) collective-permute-start(f32[3,70,512]{2,1,0:T(8,128)S(1)} %get-tuple-element.16), channel_id=1, source_target_pairs={{8,16},{16,8},{9,17},{17,9},{10,18},{18,10},{11,19},{19,11},{12,20... | collective-permute-start | bytes 1290248 | tf_op jit(solution)/shard_map/ppermute | solution.py:100
  24.7 0.0 collective-permute-done.5
  24.7 0.1 collective-permute-start.6
  24.8 0.1 collective-permute-start.8
  24.9 4.0 %collective-permute-done.8 = f32[128,128]{1,0:T(8,128)S(1)} collective-permute-done((f32[128,128]{1,0:T(8,128)S(1)}, f32[128,128]{1,0:T(8,128)S(1)}, u32[]{:S(2)}, u32[]{:S(2)}) %collective-permute-start.8) | collective-permute-done | bytes 65568 | tf_op jit(solution)/shard_map/ppermute | solution.py:94
  28.9 0.8 collective-permute-start.9
  29.7 1.2 %collective-permute-start.10 = (f32[128,128]{1,0:T(8,128)S(1)}, f32[128,128]{1,0:T(8,128)S(1)}, u32[]{:S(2)}, u32[]{:S(2)}) collective-permute-start(f32[128,128]{1,0:T(8,128)S(1)} %add.19.p0), channel_id=1, source_target_pairs={{0,8},{8,0},{16,24},{24,16},{1,9},{9,1},{17,25},{25,17},{2,10},{10... | collective-permute-start | bytes 196616 | tf_op jit(solution)/shard_map/ppermute | solution.py:94
  30.9 1.2 %collective-permute-done.9.p1 = f32[128,128]{1,0:T(8,128)S(1)} collective-permute-done((f32[128,128]{1,0:T(8,128)S(1)}, f32[128,128]{1,0:T(8,128)S(1)}, u32[]{:S(2)}, u32[]{:S(2)}) %collective-permute-start.9) | collective-permute-done | bytes 65568 | tf_op jit(solution)/shard_map/ppermute | solution.py:94
  32.1 2.7 %collective-permute-start.11 = (f32[128,128]{1,0:T(8,128)S(1)}, f32[128,128]{1,0:T(8,128)S(1)}, u32[]{:S(2)}, u32[]{:S(2)}) collective-permute-start(f32[128,128]{1,0:T(8,128)S(1)} %collective-permute-done.9.p1), channel_id=1, source_target_pairs={{0,8},{8,0},{16,24},{24,16},{1,9},{9,1},{17,25},{25,17},{2,10},{10... | collective-permute-start | bytes 196616 | tf_op jit(solution)/shard_map/ppermute | solution.py:94
  34.8 0.8 copy.11
  35.6 0.7 reshape.3.kern
  36.3 0.0 collective-permute-done.7.rows1_ref
  36.3 0.5 copy-done.7
  36.9 0.0 copy-done.8
  36.9 0.2 copy-done.3
  37.1 0.8 copy-done.4
  37.8 47.0 %forecast.1 = f32[16,64,512]{2,1,0:T(8,128)} custom-call(s32[8]{0:T(128)} %order.3, s32[8,128]{1,0:T(8,128)} %cell_ref.1, s32[8,32]{1,0:T(8,128)} %mask.1, f32[8,49]{1,0:T(8,128)} %reshape.3.kern, f32[8,8]{1,0:T(8,128)} %mix.1, s32[8,128]{1,0:T(8,128)} %cell_ref.1, f32[8,128]{1,0:T(8,128)} %value_ref.1, f32[8,128]{1,0:T(8,128)} %var_ref.1, ...), custom_call_target="tpu_custom_call" | custom-call | tf_op jit(solution)/shard_map/forecast/pallas_call | solution.py:382
  (25 shorter events, 0.1 us)
Async XLA Ops:
  0.0 9.5 %copy-start = (f32[16,64,512]{2,1,0:T(8,128)S(1)}, f32[16,64,512]{2,1,0:T(8,128)}, u32[]{:S(2)}) copy-start(f32[16,64,512]{2,1,0:T(8,128)} %prior_ref.3) | copy-start | bytes 6291460
  2.6 1.9 %collective-permute-start = (f32[2,128,128]{2,1,0:T(8,128)}, f32[2,128,128]{2,1,0:T(8,128)S(1)}, u32[]{:S(2)}, u32[]{:S(2)}) collective-permute-start(f32[2,128,128]{2,1,0:T(8,128)} %get-tuple-element.12), channel_id=1, source_target_pairs={{0,8},{8,0},{16,24},{24,16},{1,9},{9,1},{17,25},{25,17},{2,10},{10... | collective-permute-start | bytes 393224 | tf_op jit(solution)/shard_map/ppermute | solution.py:94
  5.4 6.2 %collective-permute-start.1 = (f32[128,128]{1,0:T(8,128)S(1)}, f32[128,128]{1,0:T(8,128)S(1)}, u32[]{:S(2)}, u32[]{:S(2)}) collective-permute-start(f32[128,128]{1,0:T(8,128)S(1)} %slice_bitcast_fusion), channel_id=1, source_target_pairs={{0,16},{8,24},{16,0},{24,8},{1,17},{9,25},{17,1},{25,9},{2,18},{10... | collective-permute-start | bytes 196616 | tf_op jit(solution)/shard_map/ppermute | solution.py:94
  9.6 7.7 %collective-permute-start.3 = (f32[16,3,512]{2,1,0:T(4,128)S(1)}, f32[16,3,512]{2,1,0:T(4,128)S(1)}, u32[]{:S(2)}, u32[]{:S(2)}) collective-permute-start(f32[16,3,512]{2,1,0:T(4,128)S(1)} %get-tuple-element.14), channel_id=1, source_target_pairs={{1,2},{3,4},{5,6},{2,1},{4,3},{6,5},{9,10},{11,12},{13,14},{10,9},... | collective-permute-start | bytes 294920 | tf_op jit(solution)/shard_map/ppermute | solution.py:100
  11.7 5.1 %collective-permute-start.4 = (f32[128,128]{1,0:T(8,128)S(1)}, f32[128,128]{1,0:T(8,128)S(1)}, u32[]{:S(2)}, u32[]{:S(2)}) collective-permute-start(f32[128,128]{1,0:T(8,128)S(1)} %fusion.2), channel_id=1, source_target_pairs={{0,1},{1,0},{2,3},{3,2},{4,5},{5,4},{6,7},{7,6},{8,9},{9,8},{10,11... | collective-permute-start | bytes 196616 | tf_op jit(solution)/shard_map/ppermute | solution.py:94
  12.7 8.1 %collective-permute-start.2 = (f32[16,3,512]{2,1,0:T(4,128)S(1)}, f32[16,3,512]{2,1,0:T(4,128)S(1)}, u32[]{:S(2)}, u32[]{:S(2)}) collective-permute-start(f32[16,3,512]{2,1,0:T(4,128)S(1)} %get-tuple-element.13), channel_id=1, source_target_pairs={{0,1},{2,3},{4,5},{6,7},{1,0},{3,2},{5,4},{7,6},{8,9},{10,11},{12,... | collective-permute-start | bytes 294920 | tf_op jit(solution)/shard_map/ppermute | solution.py:100
  16.8 7.9 %collective-permute-start.5 = (f32[128,128]{1,0:T(8,128)S(1)}, f32[128,128]{1,0:T(8,128)S(1)}, u32[]{:S(2)}, u32[]{:S(2)}) collective-permute-start(f32[128,128]{1,0:T(8,128)S(1)} %add.17), channel_id=1, source_target_pairs={{0,2},{1,3},{2,0},{3,1},{4,6},{5,7},{6,4},{7,5},{8,10},{9,11},{10,... | collective-permute-start | bytes 196616 | tf_op jit(solution)/shard_map/ppermute | solution.py:94
  17.3 19.0 %copy-start.1 = (f32[16,3,512]{2,1,0:T(4,128)}, f32[16,3,512]{2,1,0:T(4,128)S(1)}, u32[]{:S(2)}) copy-start(f32[16,3,512]{2,1,0:T(4,128)S(1)} %collective-permute-done.3.side1_ref) | copy-start | bytes 294916
  20.8 15.5 %copy-start.2 = (f32[16,3,512]{2,1,0:T(4,128)}, f32[16,3,512]{2,1,0:T(4,128)S(1)}, u32[]{:S(2)}) copy-start(f32[16,3,512]{2,1,0:T(4,128)S(1)} %collective-permute-done.2.side0_ref) | copy-start | bytes 294916
  21.0 15.3 %collective-permute-start.7 = (f32[3,70,512]{2,1,0:T(8,128)S(1)}, f32[3,70,512]{2,1,0:T(8,128)S(1)}, u32[]{:S(2)}, u32[]{:S(2)}) collective-permute-start(f32[3,70,512]{2,1,0:T(8,128)S(1)} %get-tuple-element.16), channel_id=1, source_target_pairs={{8,16},{16,8},{9,17},{17,9},{10,18},{18,10},{11,19},{19,11},{12,20... | collective-permute-start | bytes 1290248 | tf_op jit(solution)/shard_map/ppermute | solution.py:100
  24.7 11.6 %collective-permute-start.6 = (f32[3,70,512]{2,1,0:T(8,128)S(1)}, f32[3,70,512]{2,1,0:T(8,128)S(1)}, u32[]{:S(2)}, u32[]{:S(2)}) collective-permute-start(f32[3,70,512]{2,1,0:T(8,128)S(1)} %get-tuple-element.15), channel_id=1, source_target_pairs={{0,8},{16,24},{8,0},{24,16},{1,9},{17,25},{9,1},{25,17},{2,10},{18... | collective-permute-start | bytes 1290248 | tf_op jit(solution)/shard_map/ppermute | solution.py:100
  24.8 4.1 %collective-permute-start.8 = (f32[128,128]{1,0:T(8,128)S(1)}, f32[128,128]{1,0:T(8,128)S(1)}, u32[]{:S(2)}, u32[]{:S(2)}) collective-permute-start(f32[128,128]{1,0:T(8,128)S(1)} %add.18), channel_id=1, source_target_pairs={{0,4},{1,5},{2,6},{3,7},{4,0},{5,1},{6,2},{7,3},{8,12},{9,13},{10,... | collective-permute-start | bytes 196616 | tf_op jit(solution)/shard_map/ppermute | solution.py:94
  28.9 7.4 %copy-start.5 = (f32[128,128]{1,0:T(8,128)}, f32[128,128]{1,0:T(8,128)S(1)}, u32[]{:S(2)}) copy-start(f32[128,128]{1,0:T(8,128)S(1)} %add.19.p0) | copy-start | bytes 196612
  28.9 3.2 %collective-permute-start.9 = (f32[128,128]{1,0:T(8,128)S(1)}, f32[128,128]{1,0:T(8,128)S(1)}, u32[]{:S(2)}, u32[]{:S(2)}) collective-permute-start(f32[128,128]{1,0:T(8,128)S(1)} %add.19.p0), channel_id=1, source_target_pairs={{0,16},{8,24},{16,0},{24,8},{1,17},{9,25},{17,1},{25,9},{2,18},{10... | collective-permute-start | bytes 196616 | tf_op jit(solution)/shard_map/ppermute | solution.py:94
  29.7 6.5 %collective-permute-start.10 = (f32[128,128]{1,0:T(8,128)S(1)}, f32[128,128]{1,0:T(8,128)S(1)}, u32[]{:S(2)}, u32[]{:S(2)}) collective-permute-start(f32[128,128]{1,0:T(8,128)S(1)} %add.19.p0), channel_id=1, source_target_pairs={{0,8},{8,0},{16,24},{24,16},{1,9},{9,1},{17,25},{25,17},{2,10},{10... | collective-permute-start | bytes 196616 | tf_op jit(solution)/shard_map/ppermute | solution.py:94
  32.1 4.2 %copy-start.6 = (f32[128,128]{1,0:T(8,128)}, f32[128,128]{1,0:T(8,128)S(1)}, u32[]{:S(2)}) copy-start(f32[128,128]{1,0:T(8,128)S(1)} %collective-permute-done.9.p1) | copy-start | bytes 196612
  32.1 4.2 %collective-permute-start.11 = (f32[128,128]{1,0:T(8,128)S(1)}, f32[128,128]{1,0:T(8,128)S(1)}, u32[]{:S(2)}, u32[]{:S(2)}) collective-permute-start(f32[128,128]{1,0:T(8,128)S(1)} %collective-permute-done.9.p1), channel_id=1, source_target_pairs={{0,8},{8,0},{16,24},{24,16},{1,9},{9,1},{17,25},{25,17},{2,10},{10... | collective-permute-start | bytes 196616 | tf_op jit(solution)/shard_map/ppermute | solution.py:94
  36.2 0.6 copy-start.7
  36.2 0.7 copy-start.8
  36.3 0.8 copy-start.3
  37.1 0.8 copy-start.4
where the time goes:
time: 85.4 us; the launch traced here: 84.9 us
  Pallas kernels  49.7 us (58%)
  starting transfers between devices  17.3 us (20%)
  waiting for transfers between devices  13.5 us (16%)
  local copies, waits for them, and re-layouts  3.03 us (4%)
  other arithmetic  1.18 us (1%)
    pallas_call x1, Pallas kernels, shards(): pl.pallas_call(functools.partial(forecast_kernel, width), out_shape=jax.S...  47 us
    ppermute x8, starting transfers between devices, flip(): lax.ppermute(x, axis, [(i, i ^ bit) for i in range(lax.axis_size(axis))])  11 us
    ppermute x8, waiting for transfers between devices, flip(): lax.ppermute(x, axis, [(i, i ^ bit) for i in range(lax.axis_size(axis))])  10 us
    ppermute x4, starting transfers between devices, swap(): return lax.ppermute(x, axis, pairs_of + [(j, i) for i, j in pairs_of])  6.24 us
    ppermute x4, waiting for transfers between devices, swap(): return lax.ppermute(x, axis, pairs_of + [(j, i) for i, j in pairs_of])  3.49 us
    pallas_call x1, Pallas kernels, shards(): pl.pallas_call(functools.partial(gather_kernel, width), out_shape=(jax.Sh...  2.61 us
    unnamed x19, local copies, waits for them, and re-layouts  2.27 us
  transfers between devices with their start and end apart: 12, of which 6 were waited for; matrix products, arithmetic and copies ran while one was open for 2% of the time, Pallas kernels for 0%

commit v1 on v0

--- a/solution.py
+++ b/solution.py
@@ -260,11 +260,11 @@
         tall = jnp.concatenate([jnp.where(low_obs, gain, zero), jnp.where(low_obs, zero, gain)], 0)
         gain_ref[...] = jnp.concatenate(split(tall), 1)
 
-    def assimilate(k, spread_ref, gain_ref, next_spread_ref, next_gain_ref):
+    def assimilate(k, waiting, spread_ref, gain_ref, next_spread_ref, next_gain_ref):
         batch = order[k]
         spread_w, gain_w = spread_ref[...], gain_ref[...]
         obs_row, obs_col = place[pl.ds(k, 1), :], place[pl.ds(8 + k, 1), :]
-        for q in range(4):
+        for q in waiting:
             halves = []
             for later in (q, q + 4):
                 dr = row_col[:, later : later + 1] - obs_row
@@ -292,11 +292,17 @@
     factors(jnp.int32(0), spread0, gain0)
 
     def two(i, carry):
-        assimilate(2 * i, spread0, gain0, spread1, gain1)
-        assimilate(2 * i + 1, spread1, gain1, spread0, gain0)
+        assimilate(2 * i, (0, 1, 2, 3), spread0, gain0, spread1, gain1)
+        assimilate(2 * i + 1, (0, 1, 2, 3), spread1, gain1, spread0, gain0)
         return carry
 
-    lax.fori_loop(0, BATCHES // 2, two, 0)
+    def last_two(i, carry):
+        assimilate(2 * i, (1, 2, 3), spread0, gain0, spread1, gain1)
+        assimilate(2 * i + 1, (2, 3), spread1, gain1, spread0, gain0)
+        return carry
+
+    lax.fori_loop(0, 2, two, 0)
+    lax.fori_loop(2, 4, last_two, 0)
 
     sources = [pairs + 2, pairs] + list(range(pairs)) + [pairs + 1, pairs + 2]
     column = lax.broadcasted_iota(jnp.int32, (cols, 3 * depth), 1)
@@ -313,7 +319,7 @@
         for a in range(KW):
             band = jnp.zeros((cols, 3 * depth), F32)
             for e in range(KW):
-                band = jnp.where(offset == e, kern[t, a * KW + e], band)
+                band = jnp.where(offset == e, kern[a, t, e], band)
             high = band.astype(BF16).astype(F32)
             bands.append(jnp.where(third, band - high, high).astype(BF16))
         band = jnp.concatenate(bands, 0)
@@ -343,7 +349,7 @@
             before = after
         return carry
 
-    lax.fori_loop(0, SPECIES, species, 0)
+    lax.fori_loop(0, SPECIES, species, 0, unroll=4)
 
     def mixed(j, carry):
         smooth = [field[j, t, 0:cols, :] for t in range(SPECIES)]
@@ -360,7 +366,7 @@
             )
         return carry
 
-    lax.fori_loop(0, pairs, mixed, 0)
+    lax.fori_loop(0, pairs, mixed, 0, unroll=2)
 
 
 def shards(prior, obs_cell, obs_weight, obs_value, obs_var, loc_mask, batch_order, kernel, mixing):
@@ -398,7 +404,7 @@
         compiler_params=PARAMS,
         name="forecast",
     )(
-        batch_order, obs_cell, loc_mask, kernel.reshape(SPECIES, KW * KW), mixing,
+        batch_order, obs_cell, loc_mask, jnp.transpose(kernel, (1, 0, 2)), mixing,
         obs_cell, obs_value, obs_var, prior, *halo, *parts,
     )
 

time: 85.4 us -> 83.6 us (0.979)
  the two profiles are of different devices: /device:TPU:9 before, /device:TPU:0 now
where the time goes in v1:
time: 83.6 us; the launch traced here: 83.4 us
  Pallas kernels  47.1 us (56%)
  starting transfers between devices  19 us (23%)
  waiting for transfers between devices  14.9 us (18%)
  other arithmetic  1.18 us (1%)
  local copies, waits for them, and re-layouts  1.01 us (1%)
    pallas_call x1, Pallas kernels, shards(): pl.pallas_call(functools.partial(forecast_kernel, width), out_shape=jax.S...  44.5 us
    ppermute x8, starting transfers between devices, flip(): lax.ppermute(x, axis, [(i, i ^ bit) for i in range(lax.axis_size(axis))])  16.8 us
    ppermute x8, waiting for transfers between devices, flip(): lax.ppermute(x, axis, [(i, i ^ bit) for i in range(lax.axis_size(axis))])  14.9 us
    pallas_call x1, Pallas kernels, shards(): pl.pallas_call(functools.partial(gather_kernel, width), out_shape=(jax.Sh...  2.61 us
    ppermute x4, starting transfers between devices, swap(): return lax.ppermute(x, axis, pairs_of + [(j, i) for i, j in pairs_of])  2.2 us
  transfers between devices with their start and end apart: 12, of which 7 were waited for; matrix products, arithmetic and copies ran while one was open for 0% of the time, Pallas kernels for 0%

profile of v1, /device:TPU:0, one launch (start us, length us, event | category | flops | bytes accessed | tf_op | source)
XLA Modules:
  0.0 83.4 jit_solution(5393288287389222031)
XLA Ops:
  0.0 2.6 %gather.1 = (f32[2,128,128]{2,1,0:T(8,128)}, f32[2,128,128]{2,1,0:T(8,128)}) custom-call(s32[8]{0:T(128)} %order.3, s32[8,128]{1,0:T(8,128)} %cell_ref.1, f32[8,8,128]{2,1,0:T(8,128)} %bitcast.8, f32[16,64,512]{2,1,0:T(8,128)} %prior_ref.3), custom_call_target="tpu_custom_call" | custom-call | tf_op jit(solution)/shard_map/gather/pallas_call | solution.py:378
  2.6 0.5 collective-permute-start
  3.1 1.2 %collective-permute-done = f32[2,128,128]{2,1,0:T(8,128)S(1)} collective-permute-done((f32[2,128,128]{2,1,0:T(8,128)}, f32[2,128,128]{2,1,0:T(8,128)S(1)}, u32[]{:S(2)}, u32[]{:S(2)}) %collective-permute-start) | collective-permute-done | bytes 131104 | tf_op jit(solution)/shard_map/ppermute | solution.py:94
  4.3 0.9 %add.15 = f32[2,128,128]{2,1,0:T(8,128)S(1)} add(f32[2,128,128]{2,1,0:T(8,128)} %get-tuple-element.11, f32[2,128,128]{2,1,0:T(8,128)S(1)} %collective-permute-done) | non-fusion elementwise | flops 32768 | bytes 393216 | tf_op jit(solution)/shard_map/add | solution.py:112
  5.2 2.9 %collective-permute-start.1 = (f32[128,128]{1,0:T(8,128)S(1)}, f32[128,128]{1,0:T(8,128)S(1)}, u32[]{:S(2)}, u32[]{:S(2)}) collective-permute-start(f32[128,128]{1,0:T(8,128)S(1)} %slice_bitcast_fusion), channel_id=1, source_target_pairs={{0,16},{8,24},{16,0},{24,8},{1,17},{9,25},{17,1},{25,9},{2,18},{10... | collective-permute-start | bytes 196616 | tf_op jit(solution)/shard_map/ppermute | solution.py:94
  8.1 0.1 slice_select_fusion
  8.2 0.7 collective-permute-start.3
  8.9 1.7 %collective-permute-done.1 = f32[128,128]{1,0:T(8,128)S(1)} collective-permute-done((f32[128,128]{1,0:T(8,128)S(1)}, f32[128,128]{1,0:T(8,128)S(1)}, u32[]{:S(2)}, u32[]{:S(2)}) %collective-permute-start.1) | collective-permute-done | bytes 65568 | tf_op jit(solution)/shard_map/ppermute | solution.py:94
  10.6 2.7 %collective-permute-start.4 = (f32[128,128]{1,0:T(8,128)S(1)}, f32[128,128]{1,0:T(8,128)S(1)}, u32[]{:S(2)}, u32[]{:S(2)}) collective-permute-start(f32[128,128]{1,0:T(8,128)S(1)} %fusion.2), channel_id=1, source_target_pairs={{0,1},{1,0},{2,3},{3,2},{4,5},{5,4},{6,7},{7,6},{8,9},{9,8},{10,11... | collective-permute-start | bytes 196616 | tf_op jit(solution)/shard_map/ppermute | solution.py:94
  13.3 0.1 collective-permute-start.2
  13.3 0.1 fusion.3
  13.4 3.4 %collective-permute-done.4 = f32[128,128]{1,0:T(8,128)S(1)} collective-permute-done((f32[128,128]{1,0:T(8,128)S(1)}, f32[128,128]{1,0:T(8,128)S(1)}, u32[]{:S(2)}, u32[]{:S(2)}) %collective-permute-start.4) | collective-permute-done | bytes 65568 | tf_op jit(solution)/shard_map/ppermute | solution.py:94
  16.8 4.4 %collective-permute-start.5 = (f32[128,128]{1,0:T(8,128)S(1)}, f32[128,128]{1,0:T(8,128)S(1)}, u32[]{:S(2)}, u32[]{:S(2)}) collective-permute-start(f32[128,128]{1,0:T(8,128)S(1)} %add.17), channel_id=1, source_target_pairs={{0,2},{1,3},{2,0},{3,1},{4,6},{5,7},{6,4},{7,5},{8,10},{9,11},{10,... | collective-permute-start | bytes 196616 | tf_op jit(solution)/shard_map/ppermute | solution.py:94
  21.2 0.0 collective-permute-done.3.side1_ref
  21.2 0.0 collective-permute-done.2.side0_ref
  21.3 0.1 fusion
  21.4 0.9 %collective-permute-start.7 = (f32[3,70,512]{2,1,0:T(8,128)S(1)}, f32[3,70,512]{2,1,0:T(8,128)S(1)}, u32[]{:S(2)}, u32[]{:S(2)}) collective-permute-start(f32[3,70,512]{2,1,0:T(8,128)S(1)} %get-tuple-element.16), channel_id=1, source_target_pairs={{8,16},{16,8},{9,17},{17,9},{10,18},{18,10},{11,19},{19,11},{12,20... | collective-permute-start | bytes 1290248 | tf_op jit(solution)/shard_map/ppermute | solution.py:100
  22.3 1.1 %collective-permute-done.5 = f32[128,128]{1,0:T(8,128)S(1)} collective-permute-done((f32[128,128]{1,0:T(8,128)S(1)}, f32[128,128]{1,0:T(8,128)S(1)}, u32[]{:S(2)}, u32[]{:S(2)}) %collective-permute-start.5) | collective-permute-done | bytes 65568 | tf_op jit(solution)/shard_map/ppermute | solution.py:94
  23.5 0.6 collective-permute-start.6
  24.0 4.6 %collective-permute-start.8 = (f32[128,128]{1,0:T(8,128)S(1)}, f32[128,128]{1,0:T(8,128)S(1)}, u32[]{:S(2)}, u32[]{:S(2)}) collective-permute-start(f32[128,128]{1,0:T(8,128)S(1)} %add.18), channel_id=1, source_target_pairs={{0,4},{1,5},{2,6},{3,7},{4,0},{5,1},{6,2},{7,3},{8,12},{9,13},{10,... | collective-permute-start | bytes 196616 | tf_op jit(solution)/shard_map/ppermute | solution.py:94
  28.7 3.7 %collective-permute-done.8 = f32[128,128]{1,0:T(8,128)S(1)} collective-permute-done((f32[128,128]{1,0:T(8,128)S(1)}, f32[128,128]{1,0:T(8,128)S(1)}, u32[]{:S(2)}, u32[]{:S(2)}) %collective-permute-start.8) | collective-permute-done | bytes 65568 | tf_op jit(solution)/shard_map/ppermute | solution.py:94
  32.4 1.7 %collective-permute-start.9 = (f32[128,128]{1,0:T(8,128)S(1)}, f32[128,128]{1,0:T(8,128)S(1)}, u32[]{:S(2)}, u32[]{:S(2)}) collective-permute-start(f32[128,128]{1,0:T(8,128)S(1)} %add.19.p0), channel_id=1, source_target_pairs={{0,16},{8,24},{16,0},{24,8},{1,17},{9,25},{17,1},{25,9},{2,18},{10... | collective-permute-start | bytes 196616 | tf_op jit(solution)/shard_map/ppermute | solution.py:94
  34.1 0.0 collective-permute-start.10
  34.1 2.6 %collective-permute-done.9.p1 = f32[128,128]{1,0:T(8,128)S(1)} collective-permute-done((f32[128,128]{1,0:T(8,128)S(1)}, f32[128,128]{1,0:T(8,128)S(1)}, u32[]{:S(2)}, u32[]{:S(2)}) %collective-permute-start.9) | collective-permute-done | bytes 65568 | tf_op jit(solution)/shard_map/ppermute | solution.py:94
  36.8 0.0 collective-permute-start.11
  36.8 1.2 %collective-permute-done.11.p3 = f32[128,128]{1,0:T(8,128)S(1)} collective-permute-done((f32[128,128]{1,0:T(8,128)S(1)}, f32[128,128]{1,0:T(8,128)S(1)}, u32[]{:S(2)}, u32[]{:S(2)}) %collective-permute-start.11) | collective-permute-done | bytes 65568 | tf_op jit(solution)/shard_map/ppermute | solution.py:94
  38.0 0.0 collective-permute-done.7.rows1_ref
  38.0 0.0 collective-permute-done.6.rows0_ref
  38.1 0.5 copy-done.8
  38.6 0.2 copy-done.3
  38.8 0.2 copy-done.4
  39.0 44.5 %forecast.1 = f32[16,64,512]{2,1,0:T(8,128)} custom-call(s32[8]{0:T(128)} %order.3, s32[8,128]{1,0:T(8,128)} %cell_ref.1, s32[8,32]{1,0:T(8,128)} %mask.1, f32[7,8,7]{2,1,0:T(8,128)} %bitcast.9, f32[8,8]{1,0:T(8,128)} %mix.1, s32[8,128]{1,0:T(8,128)} %cell_ref.1, f32[8,128]{1,0:T(8,128)} %value_ref.1, f32[8,128]{1,0:T(8,128)} %var_ref.1, ...), custom_call_target="tpu_custom_call" | custom-call | tf_op jit(solution)/shard_map/forecast/pallas_call | solution.py:388
  (23 shorter events, 0.1 us)
Async XLA Ops:
  0.0 8.1 %copy-start = (f32[16,64,512]{2,1,0:T(8,128)S(1)}, f32[16,64,512]{2,1,0:T(8,128)}, u32[]{:S(2)}) copy-start(f32[16,64,512]{2,1,0:T(8,128)} %prior_ref.3) | copy-start | bytes 6291460
  2.6 1.6 %collective-permute-start = (f32[2,128,128]{2,1,0:T(8,128)}, f32[2,128,128]{2,1,0:T(8,128)S(1)}, u32[]{:S(2)}, u32[]{:S(2)}) collective-permute-start(f32[2,128,128]{2,1,0:T(8,128)} %get-tuple-element.12), channel_id=1, source_target_pairs={{0,8},{8,0},{16,24},{24,16},{1,9},{9,1},{17,25},{25,17},{2,10},{10... | collective-permute-start | bytes 393224 | tf_op jit(solution)/shard_map/ppermute | solution.py:94
  5.2 5.3 %collective-permute-start.1 = (f32[128,128]{1,0:T(8,128)S(1)}, f32[128,128]{1,0:T(8,128)S(1)}, u32[]{:S(2)}, u32[]{:S(2)}) collective-permute-start(f32[128,128]{1,0:T(8,128)S(1)} %slice_bitcast_fusion), channel_id=1, source_target_pairs={{0,16},{8,24},{16,0},{24,8},{1,17},{9,25},{17,1},{25,9},{2,18},{10... | collective-permute-start | bytes 196616 | tf_op jit(solution)/shard_map/ppermute | solution.py:94
  8.2 13.0 %collective-permute-start.3 = (f32[16,3,512]{2,1,0:T(4,128)S(1)}, f32[16,3,512]{2,1,0:T(4,128)S(1)}, u32[]{:S(2)}, u32[]{:S(2)}) collective-permute-start(f32[16,3,512]{2,1,0:T(4,128)S(1)} %get-tuple-element.14), channel_id=1, source_target_pairs={{1,2},{3,4},{5,6},{2,1},{4,3},{6,5},{9,10},{11,12},{13,14},{10,9},... | collective-permute-start | bytes 294920 | tf_op jit(solution)/shard_map/ppermute | solution.py:100
  10.6 6.2 %collective-permute-start.4 = (f32[128,128]{1,0:T(8,128)S(1)}, f32[128,128]{1,0:T(8,128)S(1)}, u32[]{:S(2)}, u32[]{:S(2)}) collective-permute-start(f32[128,128]{1,0:T(8,128)S(1)} %fusion.2), channel_id=1, source_target_pairs={{0,1},{1,0},{2,3},{3,2},{4,5},{5,4},{6,7},{7,6},{8,9},{9,8},{10,11... | collective-permute-start | bytes 196616 | tf_op jit(solution)/shard_map/ppermute | solution.py:94
  13.3 7.9 %collective-permute-start.2 = (f32[16,3,512]{2,1,0:T(4,128)S(1)}, f32[16,3,512]{2,1,0:T(4,128)S(1)}, u32[]{:S(2)}, u32[]{:S(2)}) collective-permute-start(f32[16,3,512]{2,1,0:T(4,128)S(1)} %get-tuple-element.13), channel_id=1, source_target_pairs={{0,1},{2,3},{4,5},{6,7},{1,0},{3,2},{5,4},{7,6},{8,9},{10,11},{12,... | collective-permute-start | bytes 294920 | tf_op jit(solution)/shard_map/ppermute | solution.py:100
  16.8 6.7 %collective-permute-start.5 = (f32[128,128]{1,0:T(8,128)S(1)}, f32[128,128]{1,0:T(8,128)S(1)}, u32[]{:S(2)}, u32[]{:S(2)}) collective-permute-start(f32[128,128]{1,0:T(8,128)S(1)} %add.17), channel_id=1, source_target_pairs={{0,2},{1,3},{2,0},{3,1},{4,6},{5,7},{6,4},{7,5},{8,10},{9,11},{10,... | collective-permute-start | bytes 196616 | tf_op jit(solution)/shard_map/ppermute | solution.py:94
  21.2 16.8 %copy-start.1 = (f32[16,3,512]{2,1,0:T(4,128)}, f32[16,3,512]{2,1,0:T(4,128)S(1)}, u32[]{:S(2)}) copy-start(f32[16,3,512]{2,1,0:T(4,128)S(1)} %collective-permute-done.3.side1_ref) | copy-start | bytes 294916
  21.2 16.8 %copy-start.2 = (f32[16,3,512]{2,1,0:T(4,128)}, f32[16,3,512]{2,1,0:T(4,128)S(1)}, u32[]{:S(2)}) copy-start(f32[16,3,512]{2,1,0:T(4,128)S(1)} %collective-permute-done.2.side0_ref) | copy-start | bytes 294916
  21.4 16.6 %collective-permute-start.7 = (f32[3,70,512]{2,1,0:T(8,128)S(1)}, f32[3,70,512]{2,1,0:T(8,128)S(1)}, u32[]{:S(2)}, u32[]{:S(2)}) collective-permute-start(f32[3,70,512]{2,1,0:T(8,128)S(1)} %get-tuple-element.16), channel_id=1, source_target_pairs={{8,16},{16,8},{9,17},{17,9},{10,18},{18,10},{11,19},{19,11},{12,20... | collective-permute-start | bytes 1290248 | tf_op jit(solution)/shard_map/ppermute | solution.py:100
  23.5 14.6 %collective-permute-start.6 = (f32[3,70,512]{2,1,0:T(8,128)S(1)}, f32[3,70,512]{2,1,0:T(8,128)S(1)}, u32[]{:S(2)}, u32[]{:S(2)}) collective-permute-start(f32[3,70,512]{2,1,0:T(8,128)S(1)} %get-tuple-element.15), channel_id=1, source_target_pairs={{0,8},{16,24},{8,0},{24,16},{1,9},{17,25},{9,1},{25,17},{2,10},{18... | collective-permute-start | bytes 1290248 | tf_op jit(solution)/shard_map/ppermute | solution.py:100
  24.0 8.4 %collective-permute-start.8 = (f32[128,128]{1,0:T(8,128)S(1)}, f32[128,128]{1,0:T(8,128)S(1)}, u32[]{:S(2)}, u32[]{:S(2)}) collective-permute-start(f32[128,128]{1,0:T(8,128)S(1)} %add.18), channel_id=1, source_target_pairs={{0,4},{1,5},{2,6},{3,7},{4,0},{5,1},{6,2},{7,3},{8,12},{9,13},{10,... | collective-permute-start | bytes 196616 | tf_op jit(solution)/shard_map/ppermute | solution.py:94
  32.4 5.6 %copy-start.5 = (f32[128,128]{1,0:T(8,128)}, f32[128,128]{1,0:T(8,128)S(1)}, u32[]{:S(2)}) copy-start(f32[128,128]{1,0:T(8,128)S(1)} %add.19.p0) | copy-start | bytes 196612
  32.4 4.3 %collective-permute-start.9 = (f32[128,128]{1,0:T(8,128)S(1)}, f32[128,128]{1,0:T(8,128)S(1)}, u32[]{:S(2)}, u32[]{:S(2)}) collective-permute-start(f32[128,128]{1,0:T(8,128)S(1)} %add.19.p0), channel_id=1, source_target_pairs={{0,16},{8,24},{16,0},{24,8},{1,17},{9,25},{17,1},{25,9},{2,18},{10... | collective-permute-start | bytes 196616 | tf_op jit(solution)/shard_map/ppermute | solution.py:94
  34.1 2.6 %collective-permute-start.10 = (f32[128,128]{1,0:T(8,128)S(1)}, f32[128,128]{1,0:T(8,128)S(1)}, u32[]{:S(2)}, u32[]{:S(2)}) collective-permute-start(f32[128,128]{1,0:T(8,128)S(1)} %add.19.p0), channel_id=1, source_target_pairs={{0,8},{8,0},{16,24},{24,16},{1,9},{9,1},{17,25},{25,17},{2,10},{10... | collective-permute-start | bytes 196616 | tf_op jit(solution)/shard_map/ppermute | solution.py:94
  36.8 1.3 %copy-start.6 = (f32[128,128]{1,0:T(8,128)}, f32[128,128]{1,0:T(8,128)S(1)}, u32[]{:S(2)}) copy-start(f32[128,128]{1,0:T(8,128)S(1)} %collective-permute-done.9.p1) | copy-start | bytes 196612
  36.8 1.3 %collective-permute-start.11 = (f32[128,128]{1,0:T(8,128)S(1)}, f32[128,128]{1,0:T(8,128)S(1)}, u32[]{:S(2)}, u32[]{:S(2)}) collective-permute-start(f32[128,128]{1,0:T(8,128)S(1)} %collective-permute-done.9.p1), channel_id=1, source_target_pairs={{0,8},{8,0},{16,24},{24,16},{1,9},{9,1},{17,25},{25,17},{2,10},{10... | collective-permute-start | bytes 196616 | tf_op jit(solution)/shard_map/ppermute | solution.py:94
  36.8 1.3 %copy-start.7 = (f32[128,128]{1,0:T(8,128)}, f32[128,128]{1,0:T(8,128)S(1)}, u32[]{:S(2)}) copy-start(f32[128,128]{1,0:T(8,128)S(1)} %collective-permute-done.10.p2) | copy-start | bytes 196612
  38.0 0.6 copy-start.8
  38.0 0.8 copy-start.3
  38.0 0.9 %copy-start.4 = (f32[3,70,512]{2,1,0:T(8,128)}, f32[3,70,512]{2,1,0:T(8,128)S(1)}, u32[]{:S(2)}) copy-start(f32[3,70,512]{2,1,0:T(8,128)S(1)} %collective-permute-done.6.rows0_ref) | copy-start | bytes 1290244

commit v2 on v1

--- a/solution.py
+++ b/solution.py
@@ -136,9 +136,9 @@
 def update(x, taper, spread_w, gain_w):
     high, low_part = split(x)
     c_high, c_low = split(dot(jnp.concatenate([high, low_part, high], 1), spread_w) * taper)
-    both = dot(c_high, gain_w)
+    both = dot(jnp.concatenate([c_high, c_low], 1), gain_w)
     lanes = 2 * MEMBERS
-    return x + (both[:, :lanes] + both[:, lanes:] + dot(c_low, gain_w[:, :lanes]))
+    return x + (both[:, :lanes] + both[:, lanes:])
 
 
 def pair_up(a, b):
@@ -147,10 +147,13 @@
 
 
 def forecast_kernel(
-    width, order, cells, mask, kern, mix, cell_ref, value_ref, var_ref, prior_ref,
+    width, order, cells, mask, kern, mix, cell_ref, value_ref, var_ref, source_ref,
     side0_ref, side1_ref, rows0_ref, rows1_ref, p0, p1, p2, p3,
     out_ref, field, predicted, table, place, spread0, gain0, spread1, gain1, lines,
+    prior_ref, ready, came, done,
 ):
+    arrive = pltpu.make_async_copy(source_ref, prior_ref, came)
+    arrive.start()
     height, cols = prior_ref.shape[0], prior_ref.shape[1]
     my_row, my_col = lax.axis_index("rows"), lax.axis_index("cols")
     down, across = lax.axis_size("rows"), lax.axis_size("cols")
@@ -163,37 +166,6 @@
     even_row = lax.rem(my_row, 2) == 0
     even_col = lax.rem(my_col, 2) == 0
 
-    def put(j, p, lo, a, b):
-        first, second = pair_up(a, b)
-        field[j, 2 * p, lo : lo + a.shape[0], :] = first
-        field[j, 2 * p + 1, lo : lo + a.shape[0], :] = second
-
-    for j in range(pairs + 3):
-        for t in range(SPECIES):
-            field[j, t, cols:depth, :] = jnp.zeros((8, lanes), F32)
-    for p in range(SPECIES // 2):
-        at = slice(128 * p, 128 * (p + 1))
-
-        def left(r):
-            return jnp.where(even_col, side1_ref[r, :, at], side0_ref[r, :, at])
-
-        def right(r):
-            return jnp.where(even_col, side0_ref[r, :, at], side1_ref[r, :, at])
-
-        def above(r, lo, hi):
-            return jnp.where(even_row, rows1_ref[r, lo:hi, at], rows0_ref[r, lo:hi, at])
-
-        def below(r, lo, hi):
-            return jnp.where(even_row, rows0_ref[r, lo:hi, at], rows1_ref[r, lo:hi, at])
-
-        for j in range(pairs):
-            put(j, p, 0, prior_ref[2 * j, :, at], prior_ref[2 * j + 1, :, at])
-            put(j, p, cols, left(2 * j), left(2 * j + 1))
-            put(j, p, cols + HALO, right(2 * j), right(2 * j + 1))
-        for lo, hi in ((0, cols), (cols, cols + 2 * HALO)):
-            put(pairs, p, lo, above(1, lo, hi), above(2, lo, hi))
-            put(pairs + 1, p, lo, below(0, lo, hi), below(1, lo, hi))
-            put(pairs + 2, p, lo, above(0, lo, hi), below(2, lo, hi))
     batches = [order[k] for k in range(BATCHES)]
     tiles = []
     for k in range(BATCHES):
@@ -258,7 +230,8 @@
         wide_hi, wide_lo = split(wide)
         spread_ref[...] = jnp.concatenate([wide_hi, wide_hi, wide_lo], 0)
         tall = jnp.concatenate([jnp.where(low_obs, gain, zero), jnp.where(low_obs, zero, gain)], 0)
-        gain_ref[...] = jnp.concatenate(split(tall), 1)
+        tall_hi, tall_lo = split(tall)
+        gain_ref[...] = jnp.concatenate([jnp.concatenate([tall_hi, tall_lo], 1), jnp.concatenate([tall_hi, jnp.zeros_like(tall_lo)], 1)], 0)
 
     def assimilate(k, waiting, spread_ref, gain_ref, next_spread_ref, next_gain_ref):
         batch = order[k]
@@ -272,7 +245,8 @@
                 on = (mask[batch, tiles[later]] > 0).astype(F32)
                 halves.append(taper_weights(dr * dr + dc * dc) * on)
             predicted[q] = update(predicted[q], jnp.concatenate(halves, 1), spread_w, gain_w)
-        factors(jnp.minimum(k + 1, BATCHES - 1), next_spread_ref, next_gain_ref)
+        if next_spread_ref is not None:
+            factors(k + 1, next_spread_ref, next_gain_ref)
         gap = x_pos - obs_col
         gap = gap * gap
         active = []
@@ -290,19 +264,51 @@
             field[j] = new.reshape(SPECIES, depth, lanes)
 
     factors(jnp.int32(0), spread0, gain0)
+    arrive.wait()
+
+    def put(j, p, lo, a, b):
+        first, second = pair_up(a, b)
+        field[j, 2 * p, lo : lo + a.shape[0], :] = first
+        field[j, 2 * p + 1, lo : lo + a.shape[0], :] = second
+
+    for j in range(pairs + 3):
+        for t in range(SPECIES):
+            field[j, t, cols:depth, :] = jnp.zeros((8, lanes), F32)
+    for p in range(SPECIES // 2):
+        at = slice(128 * p, 128 * (p + 1))
+
+        def left(r):
+            return jnp.where(even_col, side1_ref[r, :, at], side0_ref[r, :, at])
+
+        def right(r):
+            return jnp.where(even_col, side0_ref[r, :, at], side1_ref[r, :, at])
+
+        def above(r, lo, hi):
+            return jnp.where(even_row, rows1_ref[r, lo:hi, at], rows0_ref[r, lo:hi, at])
+
+        def below(r, lo, hi):
+            return jnp.where(even_row, rows0_ref[r, lo:hi, at], rows1_ref[r, lo:hi, at])
+
+        for j in range(pairs):
+            put(j, p, 0, prior_ref[2 * j, :, at], prior_ref[2 * j + 1, :, at])
+            put(j, p, cols, left(2 * j), left(2 * j + 1))
+            put(j, p, cols + HALO, right(2 * j), right(2 * j + 1))
+        for lo, hi in ((0, cols), (cols, cols + 2 * HALO)):
+            put(pairs, p, lo, above(1, lo, hi), above(2, lo, hi))
+            put(pairs + 1, p, lo, below(0, lo, hi), below(1, lo, hi))
+            put(pairs + 2, p, lo, above(0, lo, hi), below(2, lo, hi))
+
 
     def two(i, carry):
         assimilate(2 * i, (0, 1, 2, 3), spread0, gain0, spread1, gain1)
         assimilate(2 * i + 1, (0, 1, 2, 3), spread1, gain1, spread0, gain0)
         return carry
 
-    def last_two(i, carry):
-        assimilate(2 * i, (1, 2, 3), spread0, gain0, spread1, gain1)
-        assimilate(2 * i + 1, (2, 3), spread1, gain1, spread0, gain0)
-        return carry
-
     lax.fori_loop(0, 2, two, 0)
-    lax.fori_loop(2, 4, last_two, 0)
+    assimilate(4, (1, 2, 3), spread0, gain0, spread1, gain1)
+    assimilate(5, (2, 3), spread1, gain1, spread0, gain0)
+    assimilate(6, (3,), spread0, gain0, spread1, gain1)
+    assimilate(7, (), spread1, gain1, None, None)
 
     sources = [pairs + 2, pairs] + list(range(pairs)) + [pairs + 1, pairs + 2]
     column = lax.broadcasted_iota(jnp.int32, (cols, 3 * depth), 1)
@@ -351,6 +357,10 @@
 
     lax.fori_loop(0, SPECIES, species, 0, unroll=4)
 
+    def leave(j):
+        rows = pl.ds(2 * j, 2)
+        return pltpu.make_async_copy(ready.at[rows], out_ref.at[rows], done.at[j])
+
     def mixed(j, carry):
         smooth = [field[j, t, 0:cols, :] for t in range(SPECIES)]
         for p in range(SPECIES // 2):
@@ -360,13 +370,16 @@
                 for t in range(1, SPECIES):
                     acc = acc + mix[s, t] * smooth[t]
                 total.append(acc)
-            out_ref[2 * j, :, 128 * p : 128 * (p + 1)] = jnp.where(low, total[0], swap_halves(total[1]))
-            out_ref[2 * j + 1, :, 128 * p : 128 * (p + 1)] = jnp.where(
+            ready[2 * j, :, 128 * p : 128 * (p + 1)] = jnp.where(low, total[0], swap_halves(total[1]))
+            ready[2 * j + 1, :, 128 * p : 128 * (p + 1)] = jnp.where(
                 low, swap_halves(total[0]), total[1]
             )
+        leave(j).start()
         return carry
 
     lax.fori_loop(0, pairs, mixed, 0, unroll=2)
+    for j in range(pairs):
+        leave(j).wait()
 
 
 def shards(prior, obs_cell, obs_weight, obs_value, obs_var, loc_mask, batch_order, kernel, mixing):
@@ -388,18 +401,22 @@
     return pl.pallas_call(
         functools.partial(forecast_kernel, width),
         out_shape=jax.ShapeDtypeStruct((height, cols, channels), F32),
-        in_specs=[SMEM] * 5 + [VMEM] * 12,
-        out_specs=VMEM,
+        in_specs=[SMEM] * 5 + [VMEM] * 3 + [pl.BlockSpec(memory_space=pl.ANY)] + [VMEM] * 8,
+        out_specs=pl.BlockSpec(memory_space=pl.ANY),
         scratch_shapes=[
             pltpu.VMEM((pairs + 3, SPECIES, cols + 8, lanes), F32),
             pltpu.VMEM((4, OBS, lanes), F32),
             pltpu.VMEM((24, OBS), F32),
             pltpu.VMEM((16, OBS), F32),
             pltpu.VMEM((3 * lanes, 2 * OBS), BF16),
-            pltpu.VMEM((2 * OBS, 2 * lanes), BF16),
+            pltpu.VMEM((4 * OBS, 2 * lanes), BF16),
             pltpu.VMEM((3 * lanes, 2 * OBS), BF16),
-            pltpu.VMEM((2 * OBS, 2 * lanes), BF16),
+            pltpu.VMEM((4 * OBS, 2 * lanes), BF16),
             pltpu.VMEM((pairs + 4, KW * cols, lanes), F32),
+            pltpu.VMEM((height, cols, channels), F32),
+            pltpu.VMEM((height, cols, channels), F32),
+            pltpu.SemaphoreType.DMA,
+            pltpu.SemaphoreType.DMA((pairs,)),
         ],
         compiler_params=PARAMS,
         name="forecast",

time: 83.6 us -> 81.4 us (0.974)
  the two profiles are of different devices: /device:TPU:0 before, /device:TPU:9 now
where the time goes in v2:
time: 81.4 us; the launch traced here: 81.8 us
  Pallas kernels  47.5 us (58%)
  starting transfers between devices  19.1 us (23%)
  waiting for transfers between devices  12.6 us (15%)
  other arithmetic  1.18 us (1%)
  local copies, waits for them, and re-layouts  1.01 us (1%)
    pallas_call x1, Pallas kernels, shards(): pl.pallas_call(functools.partial(forecast_kernel, width), out_shape=jax.S...  43.6 us
    ppermute x8, starting transfers between devices, flip(): lax.ppermute(x, axis, [(i, i ^ bit) for i in range(lax.axis_size(axis))])  11.9 us
    ppermute x8, waiting for transfers between devices, flip(): lax.ppermute(x, axis, [(i, i ^ bit) for i in range(lax.axis_size(axis))])  9.16 us
    ppermute x4, starting transfers between devices, swap(): return lax.ppermute(x, axis, pairs_of + [(j, i) for i, j in pairs_of])  7.18 us
    pallas_call x1, Pallas kernels, shards(): pl.pallas_call(functools.partial(gather_kernel, width), out_shape=(jax.Sh...  3.99 us
    ppermute x4, waiting for transfers between devices, swap(): return lax.ppermute(x, axis, pairs_of + [(j, i) for i, j in pairs_of])  3.44 us
  transfers between devices with their start and end apart: 12, of which 7 were waited for; matrix products, arithmetic and copies ran while one was open for 0% of the time, Pallas kernels for 0%

profile of v2, /device:TPU:9, one launch (start us, length us, event | category | flops | bytes accessed | tf_op | source)
XLA Modules:
  0.0 81.8 jit_solution(10547519806107451474)
XLA Ops:
  0.0 4.0 %gather.1 = (f32[2,128,128]{2,1,0:T(8,128)}, f32[2,128,128]{2,1,0:T(8,128)}) custom-call(s32[8]{0:T(128)} %order.3, s32[8,128]{1,0:T(8,128)} %cell_ref.1, f32[8,8,128]{2,1,0:T(8,128)} %bitcast.8, f32[16,64,512]{2,1,0:T(8,128)} %source_ref.1), custom_call_target="tpu_custom_call" | custom-call | tf_op jit(solution)/shard_map/gather/pallas_call | solution.py:391
  4.0 2.1 %collective-permute-start = (f32[2,128,128]{2,1,0:T(8,128)}, f32[2,128,128]{2,1,0:T(8,128)S(1)}, u32[]{:S(2)}, u32[]{:S(2)}) collective-permute-start(f32[2,128,128]{2,1,0:T(8,128)} %get-tuple-element.12), channel_id=1, source_target_pairs={{0,8},{8,0},{16,24},{24,16},{1,9},{9,1},{17,25},{25,17},{2,10},{10... | collective-permute-start | bytes 393224 | tf_op jit(solution)/shard_map/ppermute | solution.py:94
  6.1 1.2 %collective-permute-done = f32[2,128,128]{2,1,0:T(8,128)S(1)} collective-permute-done((f32[2,128,128]{2,1,0:T(8,128)}, f32[2,128,128]{2,1,0:T(8,128)S(1)}, u32[]{:S(2)}, u32[]{:S(2)}) %collective-permute-start) | collective-permute-done | bytes 131104 | tf_op jit(solution)/shard_map/ppermute | solution.py:94
  7.3 0.9 %add.15 = f32[2,128,128]{2,1,0:T(8,128)S(1)} add(f32[2,128,128]{2,1,0:T(8,128)} %get-tuple-element.11, f32[2,128,128]{2,1,0:T(8,128)S(1)} %collective-permute-done) | non-fusion elementwise | flops 32768 | bytes 393216 | tf_op jit(solution)/shard_map/add | solution.py:112
  8.2 2.7 %collective-permute-start.1 = (f32[128,128]{1,0:T(8,128)S(1)}, f32[128,128]{1,0:T(8,128)S(1)}, u32[]{:S(2)}, u32[]{:S(2)}) collective-permute-start(f32[128,128]{1,0:T(8,128)S(1)} %slice_bitcast_fusion), channel_id=1, source_target_pairs={{0,16},{8,24},{16,0},{24,8},{1,17},{9,25},{17,1},{25,9},{2,18},{10... | collective-permute-start | bytes 196616 | tf_op jit(solution)/shard_map/ppermute | solution.py:94
  10.9 0.1 slice_select_fusion
  10.9 1.9 %collective-permute-start.3 = (f32[16,3,512]{2,1,0:T(4,128)S(1)}, f32[16,3,512]{2,1,0:T(4,128)S(1)}, u32[]{:S(2)}, u32[]{:S(2)}) collective-permute-start(f32[16,3,512]{2,1,0:T(4,128)S(1)} %get-tuple-element.14), channel_id=1, source_target_pairs={{1,2},{3,4},{5,6},{2,1},{4,3},{6,5},{9,10},{11,12},{13,14},{10,9},... | collective-permute-start | bytes 294920 | tf_op jit(solution)/shard_map/ppermute | solution.py:100
  12.9 0.2 collective-permute-done.1
  13.1 0.1 collective-permute-start.4
  13.1 1.5 %collective-permute-start.2 = (f32[16,3,512]{2,1,0:T(4,128)S(1)}, f32[16,3,512]{2,1,0:T(4,128)S(1)}, u32[]{:S(2)}, u32[]{:S(2)}) collective-permute-start(f32[16,3,512]{2,1,0:T(4,128)S(1)} %get-tuple-element.13), channel_id=1, source_target_pairs={{0,1},{2,3},{4,5},{6,7},{1,0},{3,2},{5,4},{7,6},{8,9},{10,11},{12,... | collective-permute-start | bytes 294920 | tf_op jit(solution)/shard_map/ppermute | solution.py:100
  14.6 0.1 fusion.3
  14.7 1.6 %collective-permute-done.4 = f32[128,128]{1,0:T(8,128)S(1)} collective-permute-done((f32[128,128]{1,0:T(8,128)S(1)}, f32[128,128]{1,0:T(8,128)S(1)}, u32[]{:S(2)}, u32[]{:S(2)}) %collective-permute-start.4) | collective-permute-done | bytes 65568 | tf_op jit(solution)/shard_map/ppermute | solution.py:94
  16.3 2.4 %collective-permute-start.5 = (f32[128,128]{1,0:T(8,128)S(1)}, f32[128,128]{1,0:T(8,128)S(1)}, u32[]{:S(2)}, u32[]{:S(2)}) collective-permute-start(f32[128,128]{1,0:T(8,128)S(1)} %add.17), channel_id=1, source_target_pairs={{0,2},{1,3},{2,0},{3,1},{4,6},{5,7},{6,4},{7,5},{8,10},{9,11},{10,... | collective-permute-start | bytes 196616 | tf_op jit(solution)/shard_map/ppermute | solution.py:94
  18.7 3.4 %collective-permute-done.2.side0_ref = f32[16,3,512]{2,1,0:T(4,128)S(1)} collective-permute-done((f32[16,3,512]{2,1,0:T(4,128)S(1)}, f32[16,3,512]{2,1,0:T(4,128)S(1)}, u32[]{:S(2)}, u32[]{:S(2)}) %collective-permute-start.2) | collective-permute-done | bytes 98336 | tf_op jit(solution)/shard_map/ppermute | solution.py:100
  22.2 0.1 fusion
  22.3 3.7 %collective-permute-start.7 = (f32[3,70,512]{2,1,0:T(8,128)S(1)}, f32[3,70,512]{2,1,0:T(8,128)S(1)}, u32[]{:S(2)}, u32[]{:S(2)}) collective-permute-start(f32[3,70,512]{2,1,0:T(8,128)S(1)} %get-tuple-element.16), channel_id=1, source_target_pairs={{8,16},{16,8},{9,17},{17,9},{10,18},{18,10},{11,19},{19,11},{12,20... | collective-permute-start | bytes 1290248 | tf_op jit(solution)/shard_map/ppermute | solution.py:100
  26.1 0.0 collective-permute-done.5
  26.1 0.1 collective-permute-start.6
  26.2 0.1 collective-permute-start.8
  26.3 4.0 %collective-permute-done.8 = f32[128,128]{1,0:T(8,128)S(1)} collective-permute-done((f32[128,128]{1,0:T(8,128)S(1)}, f32[128,128]{1,0:T(8,128)S(1)}, u32[]{:S(2)}, u32[]{:S(2)}) %collective-permute-start.8) | collective-permute-done | bytes 65568 | tf_op jit(solution)/shard_map/ppermute | solution.py:94
  30.3 0.8 collective-permute-start.9
  31.0 1.1 %collective-permute-start.10 = (f32[128,128]{1,0:T(8,128)S(1)}, f32[128,128]{1,0:T(8,128)S(1)}, u32[]{:S(2)}, u32[]{:S(2)}) collective-permute-start(f32[128,128]{1,0:T(8,128)S(1)} %add.19.p0), channel_id=1, source_target_pairs={{0,8},{8,0},{16,24},{24,16},{1,9},{9,1},{17,25},{25,17},{2,10},{10... | collective-permute-start | bytes 196616 | tf_op jit(solution)/shard_map/ppermute | solution.py:94
  32.2 1.3 %collective-permute-done.9.p1 = f32[128,128]{1,0:T(8,128)S(1)} collective-permute-done((f32[128,128]{1,0:T(8,128)S(1)}, f32[128,128]{1,0:T(8,128)S(1)}, u32[]{:S(2)}, u32[]{:S(2)}) %collective-permute-start.9) | collective-permute-done | bytes 65568 | tf_op jit(solution)/shard_map/ppermute | solution.py:94
  33.5 2.7 %collective-permute-start.11 = (f32[128,128]{1,0:T(8,128)S(1)}, f32[128,128]{1,0:T(8,128)S(1)}, u32[]{:S(2)}, u32[]{:S(2)}) collective-permute-start(f32[128,128]{1,0:T(8,128)S(1)} %collective-permute-done.9.p1), channel_id=1, source_target_pairs={{0,8},{8,0},{16,24},{24,16},{1,9},{9,1},{17,25},{25,17},{2,10},{10... | collective-permute-start | bytes 196616 | tf_op jit(solution)/shard_map/ppermute | solution.py:94
  36.2 0.0 collective-permute-done.10.p2
  36.2 0.9 %collective-permute-done.11.p3 = f32[128,128]{1,0:T(8,128)S(1)} collective-permute-done((f32[128,128]{1,0:T(8,128)S(1)}, f32[128,128]{1,0:T(8,128)S(1)}, u32[]{:S(2)}, u32[]{:S(2)}) %collective-permute-start.11) | collective-permute-done | bytes 65568 | tf_op jit(solution)/shard_map/ppermute | solution.py:94
  37.1 0.0 collective-permute-done.7.rows1_ref
  37.1 0.0 collective-permute-done.6.rows0_ref
  37.2 0.5 copy-done.8
  37.7 0.2 copy-done.3
  37.9 0.2 copy-done.4
  38.1 43.6 %forecast.1 = f32[16,64,512]{2,1,0:T(8,128)} custom-call(s32[8]{0:T(128)} %order.3, s32[8,128]{1,0:T(8,128)} %cell_ref.1, s32[8,32]{1,0:T(8,128)} %mask.1, f32[7,8,7]{2,1,0:T(8,128)} %bitcast.9, f32[8,8]{1,0:T(8,128)} %mix.1, s32[8,128]{1,0:T(8,128)} %cell_ref.1, f32[8,128]{1,0:T(8,128)} %value_ref.1, f32[8,128]{1,0:T(8,128)} %var_ref.1, ...), custom_call_target="tpu_custom_call" | custom-call | tf_op jit(solution)/shard_map/forecast/pallas_call | solution.py:401
  (23 shorter events, 0.1 us)
Async XLA Ops:
  0.0 10.9 %copy-start = (f32[16,64,512]{2,1,0:T(8,128)S(1)}, f32[16,64,512]{2,1,0:T(8,128)}, u32[]{:S(2)}) copy-start(f32[16,64,512]{2,1,0:T(8,128)} %source_ref.1) | copy-start | bytes 6291460
  4.0 3.3 %collective-permute-start = (f32[2,128,128]{2,1,0:T(8,128)}, f32[2,128,128]{2,1,0:T(8,128)S(1)}, u32[]{:S(2)}, u32[]{:S(2)}) collective-permute-start(f32[2,128,128]{2,1,0:T(8,128)} %get-tuple-element.12), channel_id=1, source_target_pairs={{0,8},{8,0},{16,24},{24,16},{1,9},{9,1},{17,25},{25,17},{2,10},{10... | collective-permute-start | bytes 393224 | tf_op jit(solution)/shard_map/ppermute | solution.py:94
  8.2 4.9 %collective-permute-start.1 = (f32[128,128]{1,0:T(8,128)S(1)}, f32[128,128]{1,0:T(8,128)S(1)}, u32[]{:S(2)}, u32[]{:S(2)}) collective-permute-start(f32[128,128]{1,0:T(8,128)S(1)} %slice_bitcast_fusion), channel_id=1, source_target_pairs={{0,16},{8,24},{16,0},{24,8},{1,17},{9,25},{17,1},{25,9},{2,18},{10... | collective-permute-start | bytes 196616 | tf_op jit(solution)/shard_map/ppermute | solution.py:94
  10.9 7.7 %collective-permute-start.3 = (f32[16,3,512]{2,1,0:T(4,128)S(1)}, f32[16,3,512]{2,1,0:T(4,128)S(1)}, u32[]{:S(2)}, u32[]{:S(2)}) collective-permute-start(f32[16,3,512]{2,1,0:T(4,128)S(1)} %get-tuple-element.14), channel_id=1, source_target_pairs={{1,2},{3,4},{5,6},{2,1},{4,3},{6,5},{9,10},{11,12},{13,14},{10,9},... | collective-permute-start | bytes 294920 | tf_op jit(solution)/shard_map/ppermute | solution.py:100
  13.1 3.2 %collective-permute-start.4 = (f32[128,128]{1,0:T(8,128)S(1)}, f32[128,128]{1,0:T(8,128)S(1)}, u32[]{:S(2)}, u32[]{:S(2)}) collective-permute-start(f32[128,128]{1,0:T(8,128)S(1)} %fusion.2), channel_id=1, source_target_pairs={{0,1},{1,0},{2,3},{3,2},{4,5},{5,4},{6,7},{7,6},{8,9},{9,8},{10,11... | collective-permute-start | bytes 196616 | tf_op jit(solution)/shard_map/ppermute | solution.py:94
  13.1 9.0 %collective-permute-start.2 = (f32[16,3,512]{2,1,0:T(4,128)S(1)}, f32[16,3,512]{2,1,0:T(4,128)S(1)}, u32[]{:S(2)}, u32[]{:S(2)}) collective-permute-start(f32[16,3,512]{2,1,0:T(4,128)S(1)} %get-tuple-element.13), channel_id=1, source_target_pairs={{0,1},{2,3},{4,5},{6,7},{1,0},{3,2},{5,4},{7,6},{8,9},{10,11},{12,... | collective-permute-start | bytes 294920 | tf_op jit(solution)/shard_map/ppermute | solution.py:100
  16.3 9.8 %collective-permute-start.5 = (f32[128,128]{1,0:T(8,128)S(1)}, f32[128,128]{1,0:T(8,128)S(1)}, u32[]{:S(2)}, u32[]{:S(2)}) collective-permute-start(f32[128,128]{1,0:T(8,128)S(1)} %add.17), channel_id=1, source_target_pairs={{0,2},{1,3},{2,0},{3,1},{4,6},{5,7},{6,4},{7,5},{8,10},{9,11},{10,... | collective-permute-start | bytes 196616 | tf_op jit(solution)/shard_map/ppermute | solution.py:94
  18.7 18.4 %copy-start.1 = (f32[16,3,512]{2,1,0:T(4,128)}, f32[16,3,512]{2,1,0:T(4,128)S(1)}, u32[]{:S(2)}) copy-start(f32[16,3,512]{2,1,0:T(4,128)S(1)} %collective-permute-done.3.side1_ref) | copy-start | bytes 294916
  22.1 15.0 %copy-start.2 = (f32[16,3,512]{2,1,0:T(4,128)}, f32[16,3,512]{2,1,0:T(4,128)S(1)}, u32[]{:S(2)}) copy-start(f32[16,3,512]{2,1,0:T(4,128)S(1)} %collective-permute-done.2.side0_ref) | copy-start | bytes 294916
  22.3 14.8 %collective-permute-start.7 = (f32[3,70,512]{2,1,0:T(8,128)S(1)}, f32[3,70,512]{2,1,0:T(8,128)S(1)}, u32[]{:S(2)}, u32[]{:S(2)}) collective-permute-start(f32[3,70,512]{2,1,0:T(8,128)S(1)} %get-tuple-element.16), channel_id=1, source_target_pairs={{8,16},{16,8},{9,17},{17,9},{10,18},{18,10},{11,19},{19,11},{12,20... | collective-permute-start | bytes 1290248 | tf_op jit(solution)/shard_map/ppermute | solution.py:100
  26.1 11.0 %collective-permute-start.6 = (f32[3,70,512]{2,1,0:T(8,128)S(1)}, f32[3,70,512]{2,1,0:T(8,128)S(1)}, u32[]{:S(2)}, u32[]{:S(2)}) collective-permute-start(f32[3,70,512]{2,1,0:T(8,128)S(1)} %get-tuple-element.15), channel_id=1, source_target_pairs={{0,8},{16,24},{8,0},{24,16},{1,9},{17,25},{9,1},{25,17},{2,10},{18... | collective-permute-start | bytes 1290248 | tf_op jit(solution)/shard_map/ppermute | solution.py:100
  26.2 4.1 %collective-permute-start.8 = (f32[128,128]{1,0:T(8,128)S(1)}, f32[128,128]{1,0:T(8,128)S(1)}, u32[]{:S(2)}, u32[]{:S(2)}) collective-permute-start(f32[128,128]{1,0:T(8,128)S(1)} %add.18), channel_id=1, source_target_pairs={{0,4},{1,5},{2,6},{3,7},{4,0},{5,1},{6,2},{7,3},{8,12},{9,13},{10,... | collective-permute-start | bytes 196616 | tf_op jit(solution)/shard_map/ppermute | solution.py:94
  30.3 6.9 %copy-start.5 = (f32[128,128]{1,0:T(8,128)}, f32[128,128]{1,0:T(8,128)S(1)}, u32[]{:S(2)}) copy-start(f32[128,128]{1,0:T(8,128)S(1)} %add.19.p0) | copy-start | bytes 196612
  30.3 3.2 %collective-permute-start.9 = (f32[128,128]{1,0:T(8,128)S(1)}, f32[128,128]{1,0:T(8,128)S(1)}, u32[]{:S(2)}, u32[]{:S(2)}) collective-permute-start(f32[128,128]{1,0:T(8,128)S(1)} %add.19.p0), channel_id=1, source_target_pairs={{0,16},{8,24},{16,0},{24,8},{1,17},{9,25},{17,1},{25,9},{2,18},{10... | collective-permute-start | bytes 196616 | tf_op jit(solution)/shard_map/ppermute | solution.py:94
  31.0 5.2 %collective-permute-start.10 = (f32[128,128]{1,0:T(8,128)S(1)}, f32[128,128]{1,0:T(8,128)S(1)}, u32[]{:S(2)}, u32[]{:S(2)}) collective-permute-start(f32[128,128]{1,0:T(8,128)S(1)} %add.19.p0), channel_id=1, source_target_pairs={{0,8},{8,0},{16,24},{24,16},{1,9},{9,1},{17,25},{25,17},{2,10},{10... | collective-permute-start | bytes 196616 | tf_op jit(solution)/shard_map/ppermute | solution.py:94
  33.5 3.7 %copy-start.6 = (f32[128,128]{1,0:T(8,128)}, f32[128,128]{1,0:T(8,128)S(1)}, u32[]{:S(2)}) copy-start(f32[128,128]{1,0:T(8,128)S(1)} %collective-permute-done.9.p1) | copy-start | bytes 196612
  33.5 3.6 %collective-permute-start.11 = (f32[128,128]{1,0:T(8,128)S(1)}, f32[128,128]{1,0:T(8,128)S(1)}, u32[]{:S(2)}, u32[]{:S(2)}) collective-permute-start(f32[128,128]{1,0:T(8,128)S(1)} %collective-permute-done.9.p1), channel_id=1, source_target_pairs={{0,8},{8,0},{16,24},{24,16},{1,9},{9,1},{17,25},{25,17},{2,10},{10... | collective-permute-start | bytes 196616 | tf_op jit(solution)/shard_map/ppermute | solution.py:94
  36.2 1.0 %copy-start.7 = (f32[128,128]{1,0:T(8,128)}, f32[128,128]{1,0:T(8,128)S(1)}, u32[]{:S(2)}) copy-start(f32[128,128]{1,0:T(8,128)S(1)} %collective-permute-done.10.p2) | copy-start | bytes 196612
  37.1 0.6 copy-start.8
  37.1 0.8 copy-start.3
  37.1 0.9 %copy-start.4 = (f32[3,70,512]{2,1,0:T(8,128)}, f32[3,70,512]{2,1,0:T(8,128)S(1)}, u32[]{:S(2)}) copy-start(f32[3,70,512]{2,1,0:T(8,128)S(1)} %collective-permute-done.6.rows0_ref) | copy-start | bytes 1290244
